TPU v7x, 32 devices: a whole 2x2x4 slice. The times are simulated.
32 devices in a mesh: pre: 4 (over x, core), dec: 8 (over z, y).
Axes of the slice: x: 2, y: 2, z: 4, core: 2. Of those that a mesh axis runs over, the one named last changes fastest.
Arguments:
- queries: bfloat16 [16, 128, 8192], P('pre', None, 'dec'), may hold values from -6 to 6, as said below
- branch_kv: bfloat16 [16, 128, 2048], P('pre', None, 'dec'), may hold values from -6 to 6
- pool_kv: bfloat16 [16, 128, 2048], P('pre', None, 'dec'), may hold values from -6 to 6, as said below
- page_lists: int32 [16, 16], replicated, may hold values from 0 to 15, as said below
- anc_len: int32 [16], replicated, may hold values from 1025 to 2048
- dec_owner: int32 [16], replicated, may hold values from 0 to 7, as said below
- output_projection_weight: bfloat16 [8192, 8192], P('dec'), may hold values from -0.0625 to 0.0625
Outputs:
- layer_out: bfloat16 [16, 128, 8192], P('pre', None, 'dec')
- decode_pages: bfloat16 [32, 128, 2048], P('dec', None, 'pre')
Inputs may be any that keep to these rules, and one draw needn't show every extreme that they name: `queries`: floats within the range. `pool_kv`: floats within the range. `page_lists`: each branch lists distinct pages; the first half of the slots holds the same pages for every branch. `dec_owner`: the 4 branches of one prefill device (branches p * 4 on) go to distinct decode owners; one decode owner receives a branch from every prefill device.
All inputs are finite; a program needn't handle non-finite values.
Results may differ from a plain program's by a relative error of at most 0.024.
Values may be sent and summed in bfloat16 or wider, within the bound.
A program may use at most 128 MiB of HBM per device.

v0:
```python
import math

import jax
import jax.numpy as jnp
from jax import lax
from jax.sharding import PartitionSpec as P

HD = 128


def from_partner(value, axis, stride):
    mask = 2**stride
    pairs = [(source, source ^ mask) for source in range(lax.axis_size(axis))]
    return lax.ppermute(value, axis, pairs)


def page_visibility(lists, counts, page_count, page_len):
    slots = lists.shape[1]
    page_ids = jnp.arange(page_count, dtype=jnp.int32)
    reach = jnp.clip(
        counts[:, None] - jnp.arange(slots, dtype=jnp.int32)[None, :] * page_len, 0, page_len
    )
    match = lists[:, :, None] == page_ids[None, None, :]
    visible_count = jnp.sum(jnp.where(match, reach[:, :, None], 0), axis=1)
    tokens = jnp.arange(page_len, dtype=jnp.int32)
    allowed = tokens[None, None, :] < visible_count[:, :, None]
    return allowed.reshape(lists.shape[0], page_count * page_len)


def empty_state(branch_count, page_len, heads, head_size):
    return (
        jnp.zeros((branch_count, page_len, heads, head_size), jnp.float32),
        jnp.full((branch_count, page_len, heads), -jnp.inf, jnp.float32),
        jnp.zeros((branch_count, page_len, heads), jnp.float32),
    )


def merge_score_block(softmax_state, scores, values, form):
    running_output, running_maximum, running_denominator = softmax_state
    new_peak = jnp.maximum(running_maximum, jnp.max(scores, axis=-1))
    anchor = jnp.where(jnp.isfinite(new_peak), new_peak, 0.0)
    weights = jnp.exp(scores - anchor[..., None])
    shrink = jnp.exp(running_maximum - anchor)
    running_denominator = running_denominator * shrink + jnp.sum(weights, axis=-1)
    running_output = running_output * shrink[..., None] + jnp.einsum(
        form, weights.astype(jnp.bfloat16), values, preferred_element_type=jnp.float32
    )
    return (running_output, new_peak, running_denominator)


def absorb_block(softmax_state, query_vectors, keys, values, allowed, softmax_scale):
    scores = (
        jnp.einsum("bqhd,kd->bqhk", query_vectors, keys, preferred_element_type=jnp.float32)
        * softmax_scale
    )
    scores = jnp.where(allowed[:, None, None, :], scores, -jnp.inf)
    return merge_score_block(softmax_state, scores, values, "bqhk,kd->bqhd")


def absorb_pages(softmax_state, query_vectors, page_keys, page_values, allowed, softmax_scale):
    page_count, page_len, head_size = page_keys.shape
    step = math.gcd(page_count, max(1, 512 // page_len))
    blocks = page_count // step
    keys = page_keys.reshape(blocks, step * page_len, head_size)
    values = page_values.reshape(blocks, step * page_len, head_size)
    masks = allowed.reshape(allowed.shape[0], blocks, step * page_len).transpose(1, 0, 2)

    def one_block(carry, block):
        block_keys, block_values, block_mask = block
        return (
            absorb_block(carry, query_vectors, block_keys, block_values, block_mask, softmax_scale),
            None,
        )

    softmax_state, _ = lax.scan(one_block, softmax_state, (keys, values, masks))
    return softmax_state


def on_device(
    queries, branch_kv, pool_kv, page_lists, anc_len, dec_owner, output_projection_weight
):
    n_pre = lax.axis_size("pre")
    n_dec = lax.axis_size("dec")
    pre_idx = lax.axis_index("pre")
    dec_idx = lax.axis_index("dec")
    branch_count, page_len, query_cols = queries.shape
    heads = query_cols // HD
    softmax_scale = HD ** (-0.5)
    kv_cols = pool_kv.shape[2]
    if kv_cols < 2 * HD:
        other_pool, other_own = from_partner((pool_kv, branch_kv), "dec", 0)
        first_half = dec_idx % 2 == 0
        pool_keys = jnp.where(first_half, pool_kv, other_pool)
        pool_values = jnp.where(first_half, other_pool, pool_kv)
        branch_own_keys = jnp.where(first_half, branch_kv, other_own)
        branch_own_values = jnp.where(first_half, other_own, branch_kv)
    else:
        pool_keys = pool_kv[:, :, :HD]
        pool_values = pool_kv[:, :, HD:]
        branch_own_keys = branch_kv[:, :, :HD]
        branch_own_values = branch_kv[:, :, HD:]
    query_vectors = queries.reshape(branch_count, page_len, heads, HD)
    my_lists = lax.dynamic_slice_in_dim(page_lists, pre_idx * branch_count, branch_count, 0)
    my_counts = lax.dynamic_slice_in_dim(anc_len, pre_idx * branch_count, branch_count, 0)
    piece_keys = lax.all_gather(pool_keys, "pre", axis=0, tiled=True)
    piece_values = lax.all_gather(pool_values, "pre", axis=0, tiled=True)
    allowed = page_visibility(my_lists, my_counts, piece_keys.shape[0], page_len)
    softmax_state = absorb_pages(
        empty_state(branch_count, page_len, heads, HD),
        query_vectors,
        piece_keys,
        piece_values,
        allowed,
        softmax_scale,
    )
    causal = (
        jnp.arange(page_len, dtype=jnp.int32)[None, :]
        <= jnp.arange(page_len, dtype=jnp.int32)[:, None]
    )
    branch_own_scores = (
        jnp.einsum(
            "lntm,lpm->lntp", query_vectors, branch_own_keys, preferred_element_type=jnp.float32
        )
        * softmax_scale
    )
    branch_own_scores = jnp.where(causal[None, :, None, :], branch_own_scores, -jnp.inf)
    running_output, running_maximum, running_denominator = merge_score_block(
        softmax_state, branch_own_scores, branch_own_values, "esju,euw->esjw"
    )
    attention_result = (
        (running_output / running_denominator[..., None])
        .astype(jnp.bfloat16)
        .reshape(branch_count, page_len, heads * HD)
    )
    exponent_term = jnp.einsum(
        "oza,ae->oze",
        attention_result,
        output_projection_weight,
        preferred_element_type=jnp.float32,
    )
    layer_out = lax.psum_scatter(
        exponent_term.astype(jnp.bfloat16), "dec", scatter_dimension=2, tiled=True
    )
    owners = lax.dynamic_slice_in_dim(dec_owner, pre_idx * branch_count, branch_count, 0)
    onehot = (owners[:, None] == jnp.arange(n_dec, dtype=jnp.int32)[None, :]).astype(jnp.bfloat16)
    buckets = jnp.einsum(
        "bo,bqc->oqc", onehot, branch_kv, preferred_element_type=jnp.float32
    ).astype(jnp.bfloat16)
    buckets = buckets[:, :, None, :]
    moved = lax.all_to_all(
        lax.all_to_all(buckets, "dec", split_axis=0, concat_axis=2, tiled=True),
        "pre",
        split_axis=2,
        concat_axis=0,
        tiled=True,
    )
    decode_pages = moved.reshape(n_pre, page_len, n_dec // n_pre * kv_cols)
    return (layer_out, decode_pages)


def solution(mesh):
    in_specs = (
        P("pre", None, "dec"),
        P("pre", None, "dec"),
        P("pre", None, "dec"),
        P(),
        P(),
        P(),
        P("dec", None),
    )
    out_specs = (P("pre", None, "dec"), P("dec", None, "pre"))
    return jax.shard_map(
        on_device, mesh=mesh, in_specs=in_specs, out_specs=out_specs, check_vma=False
    )
```

profile of v0, /device:TPU:0, one launch (start us, length us, event | category | flops | bytes accessed | tf_op | source)
XLA Modules:
  0.0 275.1 jit_solution(3896425364281672524)
XLA Ops:
  7.2 0.0 copy-start
  7.2 0.0 reduce-scatter.2.cloned.1.call-start
  7.3 0.7 dynamic_slice.21
  8.0 0.0 copy-done
  8.0 0.1 subtract_clamp_fusion
  8.1 0.1 select_reduce_fusion
  8.2 0.1 lt.32
  8.4 0.0 copy-start.3
  8.4 1.7 copy.41
  10.0 0.7 copy.43
  10.7 0.0 copy-done.3
  10.8 8.6 %all_gather.6 = bf16[16,128,128]{2,1,0:T(8,128)(2,1)S(1)} all-gather(bf16[4,128,128]{2,1,0:T(8,128)(2,1)S(1)} %get-tuple-element.125), channel_id=1, replica_groups=mesh['pre'=4,'dec'=8] {'pre'}, dimensions={0}, use_global_device_ids=true | all-gather | bytes 655360 | tf_op jit(solution)/shard_map/all_gather | solution.py:105
  19.4 7.3 %all_gather.7 = bf16[16,128,128]{2,1,0:T(8,128)(2,1)S(1)} all-gather(bf16[4,128,128]{2,1,0:T(8,128)(2,1)S(1)} %get-tuple-element.124), channel_id=1, replica_groups=mesh['pre'=4,'dec'=8] {'pre'}, dimensions={0}, use_global_device_ids=true | all-gather | bytes 655360 | tf_op jit(solution)/shard_map/all_gather | solution.py:106
  26.7 59.4 %while.15 = (s32[]{:T(128)}, f32[4,128,8,128]{3,1,2,0:T(8,128)}, f32[4,128,8]{1,2,0:T(8,128)S(1)}, f32[4,128,8]{1,2,0:T(8,128)S(1)}, pred[4,4,512]{2,1,0:T(4,128...) while((s32[]{:T(128)}, f32[4,128,8,128]{3,1,2,0:T(8,128)}, ...), condition=%wide.region_4.5_spmd.clone, body=%wide.region_1.4_spmd.clone.sunk | while | flops 1098420224 | bytes 64514196 | solution.py:75
  26.7 4.0 %fusion.58 = (f32[4,128,8]{1,2,0:T(8,128)S(1)}, f32[512,4,128,8]{2,0,3,1:T(8,128)}) fusion(pred[4,512]{1,0:T(4,128)(4,1)S(1)} %dynamic-slice_bitcast_fusion.2, bf16[4,128,8,128]{3,1,2,0:T(8,128)(2,1)S(1)} %get-tuple-element.215, bf16[4,512,128]{2,1,0:T(8,128)(2,1)S(1)} %get-tuple-element.214, s32[]{:T(128)} %get-tuple-element.199), kind=kOutput, calls=%fused_computation.4.clone.1 | convolution fusion | flops 543158272 | bytes 9586692 | tf_op jit(solution)/shard_map/while/body/eval_jaxpr/bqhd,kd->bqhk/dot_general | solution.py:53
  30.6 0.0 copy-start.1
  30.7 4.8 %fusion.59 = f32[4,128,8]{1,2,0:T(8,128)S(1)} fusion(f32[512,4,128,8]{2,0,3,1:T(8,128)} %get-tuple-element.183, f32[4,128,8]{1,2,0:T(8,128)S(1)} %get-tuple-element.185, pred[4,512]{1,0:T(4,128)(4,1)S(1)} %dynamic-slice_bitcast_fusion.2), kind=kLoop, calls=%fused_computation.2.clone.1 | loop fusion | flops 8384512 | bytes 8423424 | tf_op jit(solution)/shard_map/while/body/eval_jaxpr/reduce_sum | solution.py:44
  35.5 1.0 copy-done.1
  36.5 4.0 %fusion.61 = f32[4,128,8,128]{3,1,2,0:T(8,128)} fusion(f32[4,128,8,128]{3,1,2,0:T(8,128)} %get-tuple-element.200, f32[512,4,128,8]{2,0,3,1:T(8,128)S(1)} %copy-done.1, f32[4,128,8]{1,2,0:T(8,128)S(1)} %get-tuple-element.185, pred[4,512]{1,0:T(4,128)(4,1)S(1)} %dynamic-slice_bitcast_fusion.2, f32[4,128,8]{1,2,0:T(8,128)S(1)} %get-tuple-element.187, ...), kind=kOutput, calls=%fused_computation.8.clone.1 | convolution fusion | flops 546832384 | bytes 12748805 | tf_op jit(solution)/shard_map/while/body/eval_jaxpr/bqhk,kd->bqhd/dot_general | solution.py:45
  40.4 4.0 %fusion.58 = (f32[4,128,8]{1,2,0:T(8,128)S(1)}, f32[512,4,128,8]{2,0,3,1:T(8,128)}) fusion(pred[4,512]{1,0:T(4,128)(4,1)S(1)} %dynamic-slice_bitcast_fusion.2, bf16[4,128,8,128]{3,1,2,0:T(8,128)(2,1)S(1)} %get-tuple-element.215, bf16[4,512,128]{2,1,0:T(8,128)(2,1)S(1)} %get-tuple-element.214, s32[]{:T(128)} %get-tuple-element.199), kind=kOutput, calls=%fused_computation.4.clone.1 | convolution fusion | flops 543158272 | bytes 9586692 | tf_op jit(solution)/shard_map/while/body/eval_jaxpr/bqhd,kd->bqhk/dot_general | solution.py:53
  44.4 0.0 copy-start.1
  44.4 4.8 %fusion.59 = f32[4,128,8]{1,2,0:T(8,128)S(1)} fusion(f32[512,4,128,8]{2,0,3,1:T(8,128)} %get-tuple-element.183, f32[4,128,8]{1,2,0:T(8,128)S(1)} %get-tuple-element.185, pred[4,512]{1,0:T(4,128)(4,1)S(1)} %dynamic-slice_bitcast_fusion.2), kind=kLoop, calls=%fused_computation.2.clone.1 | loop fusion | flops 8384512 | bytes 8423424 | tf_op jit(solution)/shard_map/while/body/eval_jaxpr/reduce_sum | solution.py:44
  49.3 1.0 copy-done.1
  50.2 5.4 %fusion.61 = f32[4,128,8,128]{3,1,2,0:T(8,128)} fusion(f32[4,128,8,128]{3,1,2,0:T(8,128)} %get-tuple-element.200, f32[512,4,128,8]{2,0,3,1:T(8,128)S(1)} %copy-done.1, f32[4,128,8]{1,2,0:T(8,128)S(1)} %get-tuple-element.185, pred[4,512]{1,0:T(4,128)(4,1)S(1)} %dynamic-slice_bitcast_fusion.2, f32[4,128,8]{1,2,0:T(8,128)S(1)} %get-tuple-element.187, ...), kind=kOutput, calls=%fused_computation.8.clone.1 | convolution fusion | flops 546832384 | bytes 12748805 | tf_op jit(solution)/shard_map/while/body/eval_jaxpr/bqhk,kd->bqhd/dot_general | solution.py:45
  55.7 4.0 %fusion.58 = (f32[4,128,8]{1,2,0:T(8,128)S(1)}, f32[512,4,128,8]{2,0,3,1:T(8,128)}) fusion(pred[4,512]{1,0:T(4,128)(4,1)S(1)} %dynamic-slice_bitcast_fusion.2, bf16[4,128,8,128]{3,1,2,0:T(8,128)(2,1)S(1)} %get-tuple-element.215, bf16[4,512,128]{2,1,0:T(8,128)(2,1)S(1)} %get-tuple-element.214, s32[]{:T(128)} %get-tuple-element.199), kind=kOutput, calls=%fused_computation.4.clone.1 | convolution fusion | flops 543158272 | bytes 9586692 | tf_op jit(solution)/shard_map/while/body/eval_jaxpr/bqhd,kd->bqhk/dot_general | solution.py:53
  59.6 0.0 copy-start.1
  59.6 4.8 %fusion.59 = f32[4,128,8]{1,2,0:T(8,128)S(1)} fusion(f32[512,4,128,8]{2,0,3,1:T(8,128)} %get-tuple-element.183, f32[4,128,8]{1,2,0:T(8,128)S(1)} %get-tuple-element.185, pred[4,512]{1,0:T(4,128)(4,1)S(1)} %dynamic-slice_bitcast_fusion.2), kind=kLoop, calls=%fused_computation.2.clone.1 | loop fusion | flops 8384512 | bytes 8423424 | tf_op jit(solution)/shard_map/while/body/eval_jaxpr/reduce_sum | solution.py:44
  64.5 1.0 copy-done.1
  65.5 5.4 %fusion.61 = f32[4,128,8,128]{3,1,2,0:T(8,128)} fusion(f32[4,128,8,128]{3,1,2,0:T(8,128)} %get-tuple-element.200, f32[512,4,128,8]{2,0,3,1:T(8,128)S(1)} %copy-done.1, f32[4,128,8]{1,2,0:T(8,128)S(1)} %get-tuple-element.185, pred[4,512]{1,0:T(4,128)(4,1)S(1)} %dynamic-slice_bitcast_fusion.2, f32[4,128,8]{1,2,0:T(8,128)S(1)} %get-tuple-element.187, ...), kind=kOutput, calls=%fused_computation.8.clone.1 | convolution fusion | flops 546832384 | bytes 12748805 | tf_op jit(solution)/shard_map/while/body/eval_jaxpr/bqhk,kd->bqhd/dot_general | solution.py:45
  70.9 4.0 %fusion.58 = (f32[4,128,8]{1,2,0:T(8,128)S(1)}, f32[512,4,128,8]{2,0,3,1:T(8,128)}) fusion(pred[4,512]{1,0:T(4,128)(4,1)S(1)} %dynamic-slice_bitcast_fusion.2, bf16[4,128,8,128]{3,1,2,0:T(8,128)(2,1)S(1)} %get-tuple-element.215, bf16[4,512,128]{2,1,0:T(8,128)(2,1)S(1)} %get-tuple-element.214, s32[]{:T(128)} %get-tuple-element.199), kind=kOutput, calls=%fused_computation.4.clone.1 | convolution fusion | flops 543158272 | bytes 9586692 | tf_op jit(solution)/shard_map/while/body/eval_jaxpr/bqhd,kd->bqhk/dot_general | solution.py:53
  74.8 0.0 copy-start.1
  74.8 4.8 %fusion.59 = f32[4,128,8]{1,2,0:T(8,128)S(1)} fusion(f32[512,4,128,8]{2,0,3,1:T(8,128)} %get-tuple-element.183, f32[4,128,8]{1,2,0:T(8,128)S(1)} %get-tuple-element.185, pred[4,512]{1,0:T(4,128)(4,1)S(1)} %dynamic-slice_bitcast_fusion.2), kind=kLoop, calls=%fused_computation.2.clone.1 | loop fusion | flops 8384512 | bytes 8423424 | tf_op jit(solution)/shard_map/while/body/eval_jaxpr/reduce_sum | solution.py:44
  79.7 1.0 copy-done.1
  80.7 5.4 %fusion.61 = f32[4,128,8,128]{3,1,2,0:T(8,128)} fusion(f32[4,128,8,128]{3,1,2,0:T(8,128)} %get-tuple-element.200, f32[512,4,128,8]{2,0,3,1:T(8,128)S(1)} %copy-done.1, f32[4,128,8]{1,2,0:T(8,128)S(1)} %get-tuple-element.185, pred[4,512]{1,0:T(4,128)(4,1)S(1)} %dynamic-slice_bitcast_fusion.2, f32[4,128,8]{1,2,0:T(8,128)S(1)} %get-tuple-element.187, ...), kind=kOutput, calls=%fused_computation.8.clone.1 | convolution fusion | flops 546832384 | bytes 12748805 | tf_op jit(solution)/shard_map/while/body/eval_jaxpr/bqhk,kd->bqhd/dot_general | solution.py:45
  86.1 0.0 copy-start.2
  86.1 2.0 copy.45
  88.0 0.0 copy-done.2
  88.0 0.4 fusion.24
  88.5 0.5 fusion.25
  89.0 0.8 divide_convert_fusion
  89.9 16.9 %fusion.21 = bf16[4,128,8192]{2,1,0:T(8,128)(2,1)} fusion(bf16[4,128,1024]{1,2,0:T(8,128)(2,1)S(1)} %bitcast.95, bf16[1024,8192]{1,0:T(8,128)(2,1)} %param.15), kind=kOutput, calls=%fused_computation.26 | convolution fusion | flops 8594128896 | bytes 26214400 | tf_op jit(solution)/shard_map/oza,ae->oze/dot_general | solution.py:135
  106.8 0.0 copy-start.4
  106.8 0.0 reduce-scatter.2.cloned.1.call-update
  106.8 0.6 copy-done.4
  107.5 0.1 dynamic_slice.22
  107.5 0.4 fusion.27
  108.0 0.1 copy.50
  108.1 34.8 %all_to_all.33 = bf16[8,128,1,256]{3,1,2,0:T(8,128)(2,1)S(1)} all-to-all(bf16[8,128,1,256]{3,1,2,0:T(8,128)(2,1)S(1)} %copy.50), channel_id=1, replica_groups=mesh['pre'=4,'dec'=8] {'dec'}, dimensions={0} | all-to-all | bytes 1048576 | tf_op jit(solution)/shard_map/all_to_all | solution.py:151
  142.9 11.2 %all_to_all.34 = bf16[1,128,8,256]{3,1,0,2:T(8,128)(2,1)S(1)} all-to-all(bf16[1,128,8,256]{3,1,0,2:T(8,128)(2,1)S(1)} %bitcast.92), channel_id=1, replica_groups=mesh['pre'=4,'dec'=8] {'pre'}, dimensions={2} | all-to-all | bytes 1048576 | tf_op jit(solution)/shard_map/all_to_all | solution.py:150
  154.1 0.5 copy.52
  154.7 1.1 reshape.83
  155.8 112.5 %reduce-scatter.2.cloned.1.call-done = bf16[4,128,1024]{2,1,0:T(8,128)(2,1)} async-done(((bf16[4,128,8192]{2,1,0:T(8,128)(2,1)}), bf16[4,128,1024]{2,1,0:T(8,128)(2,1)}) %reduce-scatter.2.cloned.1.call-update) | async-done | bytes 1048592 | tf_op jit(solution)/shard_map/reduce_scatter | solution.py:141
  (29 shorter events, 0.3 us)
Async XLA Ops:
  7.2 0.9 copy-start
  7.2 261.1 %reduce-scatter.2.cloned.1.call-start = ((), (), s32[]{:S(2)}) async-start(), calls=%async_computation.3 | async-start | bytes 9437184 | tf_op jit(solution)/shard_map/reduce_scatter | solution.py:141
  8.4 2.4 copy-start.3
  30.6 5.8 %copy-start.1 = (f32[512,4,128,8]{2,0,3,1:T(8,128)S(1)}, f32[512,4,128,8]{2,0,3,1:T(8,128)}, u32[]{:S(2)}) copy-start(f32[512,4,128,8]{2,0,3,1:T(8,128)} %get-tuple-element.183) | copy-start | bytes 25165828 | tf_op jit(solution)/shard_map/while
  44.4 5.8 %copy-start.1 = (f32[512,4,128,8]{2,0,3,1:T(8,128)S(1)}, f32[512,4,128,8]{2,0,3,1:T(8,128)}, u32[]{:S(2)}) copy-start(f32[512,4,128,8]{2,0,3,1:T(8,128)} %get-tuple-element.183) | copy-start | bytes 25165828 | tf_op jit(solution)/shard_map/while
  59.6 5.8 %copy-start.1 = (f32[512,4,128,8]{2,0,3,1:T(8,128)S(1)}, f32[512,4,128,8]{2,0,3,1:T(8,128)}, u32[]{:S(2)}) copy-start(f32[512,4,128,8]{2,0,3,1:T(8,128)} %get-tuple-element.183) | copy-start | bytes 25165828 | tf_op jit(solution)/shard_map/while
  74.8 5.8 %copy-start.1 = (f32[512,4,128,8]{2,0,3,1:T(8,128)S(1)}, f32[512,4,128,8]{2,0,3,1:T(8,128)}, u32[]{:S(2)}) copy-start(f32[512,4,128,8]{2,0,3,1:T(8,128)} %get-tuple-element.183) | copy-start | bytes 25165828 | tf_op jit(solution)/shard_map/while
  86.1 2.0 copy-start.2
  106.8 0.7 copy-start.4
Sparse Core Ops, SparseCore 0:
  107.0 161.2 reduce-scatter.1
where the time goes:
time: 276 us; the launch traced here: 275 us
  waiting for transfers between devices  113 us (41%)
  blocking collectives  61.9 us (22%)
  matrix products  54.6 us (20%)
  other arithmetic  20.1 us (7%)
  between operations  14.2 us (5%)
  local copies, waits for them, and re-layouts  11.6 us (4%)
    reduce_scatter x1, waiting for transfers between devices, on_device(): lax.psum_scatter(exponent_term.astype(jnp.bfloat16), 'dec', scatter_dimen...  113 us
    all_to_all x1, blocking collectives, on_device(): lax.all_to_all(buckets, 'dec', split_axis=0, concat_axis=2, tiled=True)  34.8 us
    dot_general x5, matrix products, merge_score_block(): jnp.einsum(form, weights.astype(jnp.bfloat16), values, preferred_element_...  21 us
    reduce_sum x5, other arithmetic, merge_score_block(): jnp.sum(weights, axis=-1)  19.7 us
    dot_general x1, matrix products, on_device(): jnp.einsum('oza,ae->oze', attention_result, output_projection_weight, pre...  16.9 us
    dot_general x4, matrix products, absorb_block(): jnp.einsum('bqhd,kd->bqhk', query_vectors, keys, preferred_element_type=j...  15.8 us
    all_to_all x1, blocking collectives, on_device(): lax.all_to_all(lax.all_to_all(buckets, 'dec', split_axis=0, concat_axis=2...  11.2 us
    all_gather x1, blocking collectives, on_device(): piece_keys = lax.all_gather(pool_keys, 'pre', axis=0, tiled=True)  8.65 us
  transfers between devices with their start and end apart: 1, of which 1 were waited for; matrix products, arithmetic and copies ran while one was open for 1% of the time, Pallas kernels for 0%

commit v1 on v0

v1 whole, which is shorter than its diff:
```python
import functools
import math

import jax
import jax.numpy as jnp
from jax import lax
from jax.experimental import pallas as pl
from jax.experimental.pallas import tpu as pltpu
from jax.sharding import PartitionSpec as P

HD = 128
MASKED = -1e30
SCALE = HD**-0.5 * math.log2(math.e)
FUSED = False
MESH = pl.DeviceIdType.MESH
VMEM = pl.BlockSpec(memory_space=pltpu.VMEM)


def from_partner(value, axis, stride):
    mask = 2**stride
    pairs = [(source, source ^ mask) for source in range(lax.axis_size(axis))]
    return lax.ppermute(value, axis, pairs)


def visibility_bias(lists, counts, page_count, page_len):
    slots = lists.shape[1]
    page_ids = jnp.arange(page_count, dtype=jnp.int32)
    reach = jnp.clip(
        counts[:, None] - jnp.arange(slots, dtype=jnp.int32)[None, :] * page_len, 0, page_len
    )
    match = lists[:, :, None] == page_ids[None, None, :]
    visible_count = jnp.sum(jnp.where(match, reach[:, :, None], 0), axis=1)
    tokens = jnp.arange(page_len, dtype=jnp.int32)
    allowed = tokens[None, None, :] < visible_count[:, :, None]
    allowed = allowed.reshape(lists.shape[0], 1, page_count * page_len)
    return jnp.where(allowed, 0.0, MASKED).astype(jnp.float32)


def exchange_kernel(
    n_pre, n_dec, pool_ref, bucket_ref, all_ref, pages_ref, own_sem, psend, precv, bsend, brecv
):
    pre = lax.axis_index("pre")
    dec = lax.axis_index("dec")
    count = pool_ref.shape[0]
    cols = bucket_ref.shape[2]
    ratio = n_dec // n_pre
    mine = pl.ds(pre * count, count)

    def pool_copy(k):
        return pltpu.make_async_remote_copy(
            src_ref=pool_ref,
            dst_ref=all_ref.at[mine],
            send_sem=psend.at[k],
            recv_sem=precv.at[k],
            device_id={"pre": lax.rem(pre + k, n_pre)},
            device_id_type=MESH,
        )

    for k in range(1, n_pre):
        pool_copy(k).start()
    own = pltpu.make_async_copy(pool_ref, all_ref.at[mine], own_sem)
    own.start()

    home = dec // ratio
    part = lax.rem(dec, ratio)
    column = pl.multiple_of(part * cols, 128)

    def bucket_copy(k):
        owner = lax.rem(dec + k, n_dec)
        return pltpu.make_async_remote_copy(
            src_ref=bucket_ref.at[owner],
            dst_ref=pages_ref.at[pre, :, pl.ds(column, cols)],
            send_sem=bsend.at[k],
            recv_sem=brecv.at[pre, part],
            device_id={"pre": home, "dec": owner},
            device_id_type=MESH,
        )

    for k in range(1, n_dec):
        bucket_copy(k).start()

    @pl.when(home == pre)
    def _():
        pltpu.make_async_copy(
            bucket_ref.at[dec], pages_ref.at[pre, :, pl.ds(column, cols)], brecv.at[pre, part]
        ).start()

    @pl.when(home != pre)
    def _():
        bucket_copy(0).start()

    own.wait()
    for k in range(1, n_pre):
        pool_copy(k).wait()
    for k in range(1, n_dec):
        bucket_copy(k).wait_send()

    @pl.when(home != pre)
    def _():
        bucket_copy(0).wait_send()

    for source in range(n_pre):
        for piece in range(ratio):
            place = pages_ref.at[source, :, pl.ds(piece * cols, cols)]
            pltpu.make_async_copy(place, place, brecv.at[source, piece]).wait()


def exchange(pool, buckets, n_pre, n_dec):
    count, page_len, width = pool.shape
    cols = buckets.shape[2]
    ratio = n_dec // n_pre
    return pl.pallas_call(
        functools.partial(exchange_kernel, n_pre, n_dec),
        out_shape=(
            jax.ShapeDtypeStruct((count * n_pre, page_len, width), pool.dtype),
            jax.ShapeDtypeStruct((n_pre, page_len, ratio * cols), buckets.dtype),
        ),
        in_specs=[VMEM] * 2,
        out_specs=(VMEM, VMEM),
        scratch_shapes=[
            pltpu.SemaphoreType.DMA,
            pltpu.SemaphoreType.DMA((n_pre,)),
            pltpu.SemaphoreType.DMA((n_pre,)),
            pltpu.SemaphoreType.DMA((n_dec,)),
            pltpu.SemaphoreType.DMA((n_pre, ratio)),
        ],
        compiler_params=pltpu.CompilerParams(has_side_effects=True),
        name="exchange",
    )(pool, buckets)


def load_values(pool_ref, values):
    pages, page_len, _ = pool_ref.shape
    values[:, :HD] = pool_ref[:, :, HD:].reshape(pages * page_len, HD)
    values[:, HD:] = jnp.ones((pages * page_len, HD), values.dtype)


def attend(branch, q_ref, own_ref, pool_ref, bias_ref, values, result_ref):
    pages, page_len, _ = pool_ref.shape
    heads = q_ref.shape[2] // HD
    pair = 2
    keys = pool_ref[:, :, :HD].reshape(pages * page_len, HD)
    own_keys = own_ref[branch, :, :HD]
    own_values = own_ref[branch, :, HD:]
    own_values = jnp.concatenate([own_values, jnp.ones_like(own_values)], 1)
    row = lax.broadcasted_iota(jnp.int32, (page_len, page_len), 0)
    col = lax.broadcasted_iota(jnp.int32, (page_len, page_len), 1)
    causal = jnp.where(col <= row, 0.0, MASKED)
    causal = jnp.concatenate([causal] * pair, 0)
    bias = bias_ref[branch]
    nt = (((1,), (1,)), ((), ()))

    def group(g, carry):
        start = pl.multiple_of(g * pair * HD, pair * HD)
        q = q_ref[branch, :, pl.ds(start, pair * HD)]
        q = jnp.concatenate([q[:, i * HD : (i + 1) * HD] for i in range(pair)], 0)
        far = lax.dot_general(q, keys, nt, preferred_element_type=jnp.float32) + bias
        near = lax.dot_general(q, own_keys, nt, preferred_element_type=jnp.float32) + causal
        top = jnp.maximum(
            jnp.max(far, axis=-1, keepdims=True), jnp.max(near, axis=-1, keepdims=True)
        )
        top = top * SCALE
        far = jnp.exp2(far * SCALE - top).astype(jnp.bfloat16)
        near = jnp.exp2(near * SCALE - top).astype(jnp.bfloat16)
        out = jnp.dot(far, values[...], preferred_element_type=jnp.float32)
        out = out + jnp.dot(near, own_values, preferred_element_type=jnp.float32)
        out = (out[:, :HD] / out[:, HD:]).astype(jnp.bfloat16)
        for i in range(pair):
            result_ref[branch, :, pl.ds(start + i * HD, HD)] = out[
                i * page_len : (i + 1) * page_len
            ]
        return carry

    lax.fori_loop(0, heads // pair, group, 0)


def attention_kernel(q_ref, own_ref, pool_ref, bias_ref, out_ref, values):
    load_values(pool_ref, values)

    def one(branch, carry):
        attend(branch, q_ref, own_ref, pool_ref, bias_ref, values, out_ref)
        return carry

    lax.fori_loop(0, q_ref.shape[0], one, 0)


def attention(queries, branch_kv, pool, bias):
    pages, page_len, _ = pool.shape
    return pl.pallas_call(
        attention_kernel,
        out_shape=jax.ShapeDtypeStruct(queries.shape, queries.dtype),
        in_specs=[VMEM] * 4,
        out_specs=VMEM,
        scratch_shapes=[pltpu.VMEM((pages * page_len, 2 * HD), jnp.bfloat16)],
        compiler_params=pltpu.CompilerParams(vmem_limit_bytes=48 * 2**20),
        name="attention",
    )(queries, branch_kv, pool, bias)


def project_kernel(n_dec, fused, *refs):
    if fused:
        q_ref, own_ref, pool_ref, bias_ref, w_ref, out_ref, values, attn, *refs = refs
    else:
        attn, w_ref, out_ref, *refs = refs
    wv, s1, r1, s2, r2, acc, wsem, s1sem, r1sem, s2sem, r2sem = refs
    branches = attn.shape[0]
    cols = out_ref.shape[2]
    half = n_dec // 2
    dec = lax.axis_index("dec")
    side = lax.rem(dec, 2)
    place = dec // 2
    partner = dec + 1 - 2 * side

    def target(t):
        return lax.rem(place + 1 + t, half)

    def load(slot, block):
        start = pl.multiple_of(block * cols, cols)
        return pltpu.make_async_copy(w_ref.at[:, pl.ds(start, cols)], wv.at[slot], wsem.at[slot])

    for t in range(half):
        load(t, 2 * target(t) + 1 - side).start()
    for t in range(half):
        load(half + t, 2 * target(t) + side).start()

    def first_copy(b, t):
        return pltpu.make_async_remote_copy(
            src_ref=s1.at[t, b],
            dst_ref=r1.at[t, b],
            send_sem=s1sem.at[t, b],
            recv_sem=r1sem.at[t, b],
            device_id={"dec": partner},
            device_id_type=MESH,
        )

    def second_copy(b, t):
        return pltpu.make_async_remote_copy(
            src_ref=s2.at[t, b],
            dst_ref=r2.at[t, b],
            send_sem=s2sem.at[t, b],
            recv_sem=r2sem.at[t, b],
            device_id={"dec": 2 * target(t) + side},
            device_id_type=MESH,
        )

    def loop(count, body):
        def step(i, carry):
            body(i)
            return carry

        lax.fori_loop(0, count, step, 0)

    def give(b):
        def one(t):
            s1[t, b] = jnp.dot(attn[b], wv[t], preferred_element_type=jnp.float32).astype(
                jnp.bfloat16
            )
            first_copy(b, t).start()

        loop(half, one)

    def take(b):
        def one(t):
            term = jnp.dot(attn[b], wv[half + t], preferred_element_type=jnp.float32)
            first_copy(b, t).wait_recv()
            s2[t, b] = (term + r1[t, b].astype(jnp.float32)).astype(jnp.bfloat16)
            second_copy(b, t).start()

        loop(half - 1, one)
        acc[b] = jnp.dot(attn[b], wv[n_dec - 1], preferred_element_type=jnp.float32)
        first_copy(b, half - 1).wait_recv()
        acc[b] += r1[half - 1, b].astype(jnp.float32)

    def finish(b):
        total = acc[b]
        for t in range(half - 1):
            second_copy(b, t).wait_recv()
            total = total + r2[t, b].astype(jnp.float32)
        out_ref[b] = total.astype(jnp.bfloat16)

    if fused:
        load_values(pool_ref, values)
        attend(0, q_ref, own_ref, pool_ref, bias_ref, values, attn)
    for slot in range(n_dec):
        load(slot, 0).wait()
    give(0)

    def middle(i):
        if fused:
            attend(i + 1, q_ref, own_ref, pool_ref, bias_ref, values, attn)
        give(i + 1)
        if fused:
            take(i)

    loop(branches - 1, middle)
    if fused:
        take(branches - 1)
    else:
        loop(branches, take)
    loop(branches, finish)

    def drain(b):
        for t in range(half):
            first_copy(b, t).wait_send()
        for t in range(half - 1):
            second_copy(b, t).wait_send()

    loop(branches, drain)


def project(inputs, weight, n_dec):
    fused = len(inputs) > 1
    branches, page_len, depth = inputs[0].shape
    cols = weight.shape[1] // n_dec
    half = n_dec // 2
    blocks = (half, branches, page_len, cols)
    head = []
    if fused:
        pages = inputs[2].shape[0]
        head = [
            pltpu.VMEM((pages * page_len, 2 * HD), jnp.bfloat16),
            pltpu.VMEM((branches, page_len, depth), jnp.bfloat16),
        ]
    return pl.pallas_call(
        functools.partial(project_kernel, n_dec, fused),
        out_shape=jax.ShapeDtypeStruct((branches, page_len, cols), jnp.bfloat16),
        in_specs=[VMEM] * len(inputs) + [pl.BlockSpec(memory_space=pl.ANY)],
        out_specs=VMEM,
        scratch_shapes=head
        + [
            pltpu.VMEM((n_dec, depth, cols), jnp.bfloat16),
            pltpu.VMEM(blocks, jnp.bfloat16),
            pltpu.VMEM(blocks, jnp.bfloat16),
            pltpu.VMEM((half - 1,) + blocks[1:], jnp.bfloat16),
            pltpu.VMEM((half - 1,) + blocks[1:], jnp.bfloat16),
            pltpu.VMEM(blocks[1:], jnp.float32),
            pltpu.SemaphoreType.DMA((n_dec,)),
            pltpu.SemaphoreType.DMA((half, branches)),
            pltpu.SemaphoreType.DMA((half, branches)),
            pltpu.SemaphoreType.DMA((half - 1, branches)),
            pltpu.SemaphoreType.DMA((half - 1, branches)),
        ],
        compiler_params=pltpu.CompilerParams(
            has_side_effects=True, vmem_limit_bytes=60 * 2**20
        ),
        name="project",
    )(*inputs, weight)


def on_device(
    queries, branch_kv, pool_kv, page_lists, anc_len, dec_owner, output_projection_weight
):
    n_pre = lax.axis_size("pre")
    n_dec = lax.axis_size("dec")
    pre_idx = lax.axis_index("pre")
    dec_idx = lax.axis_index("dec")
    branch_count, page_len, _ = queries.shape
    kv_cols = pool_kv.shape[2]
    if kv_cols < 2 * HD:
        other_pool, other_own = from_partner((pool_kv, branch_kv), "dec", 0)
        first_half = dec_idx % 2 == 0
        pool = jnp.where(
            first_half,
            jnp.concatenate([pool_kv, other_pool], 2),
            jnp.concatenate([other_pool, pool_kv], 2),
        )
        own = jnp.where(
            first_half,
            jnp.concatenate([branch_kv, other_own], 2),
            jnp.concatenate([other_own, branch_kv], 2),
        )
    else:
        pool, own = pool_kv, branch_kv

    start = pre_idx * branch_count
    my_lists = lax.dynamic_slice_in_dim(page_lists, start, branch_count, 0)
    my_counts = lax.dynamic_slice_in_dim(anc_len, start, branch_count, 0)
    owners = lax.dynamic_slice_in_dim(dec_owner, start, branch_count, 0)
    onehot = owners[:, None] == jnp.arange(n_dec, dtype=jnp.int32)[None, :]
    buckets = jnp.zeros((n_dec,) + branch_kv.shape[1:], branch_kv.dtype)
    for b in range(branch_count):
        buckets = jnp.where(onehot[b][:, None, None], branch_kv[b][None], buckets)

    pages, decode_pages = exchange(pool, buckets, n_pre, n_dec)
    bias = visibility_bias(my_lists, my_counts, pages.shape[0], page_len)
    if FUSED:
        inputs = (queries, own, pages, bias)
    else:
        inputs = (attention(queries, own, pages, bias),)
    layer_out = project(inputs, output_projection_weight, n_dec)
    return (layer_out, decode_pages)


def solution(mesh):
    in_specs = (
        P("pre", None, "dec"),
        P("pre", None, "dec"),
        P("pre", None, "dec"),
        P(),
        P(),
        P(),
        P("dec", None),
    )
    out_specs = (P("pre", None, "dec"), P("dec", None, "pre"))
    return jax.shard_map(
        on_device, mesh=mesh, in_specs=in_specs, out_specs=out_specs, check_vma=False
    )
```

time: 276 us -> 181 us (0.66)
  Pallas kernels: 0 us -> 168 us
  waiting for transfers between devices: 113 us -> 0 us
  blocking collectives: 61.9 us -> 0 us
  matrix products: 54.6 us -> 0 us
  other arithmetic: 20.1 us -> 2.03 us
  between operations: 14.2 us -> 0.7 us
    pallas_call x0 -> x3, Pallas kernels: none -> 168 us  [the longest x1 114 us: project(): pl.pallas_call(functools.partial(project_kernel, n_dec, fused), out_shape...]
    reduce_scatter x1 -> x0, waiting for transfers between devices: 113 us -> none  [on_device(): lax.psum_scatter(exponent_term.astype(jnp.bfloat16), 'dec', scatter_dimen...]
    dot_general x12 -> x0, matrix products: 54.6 us -> none  [the longest x5 21 us: merge_score_block(): jnp.einsum(form, weights.astype(jnp.bfloat16), values, preferred_element_...]
    all_to_all x2 -> x0, blocking collectives: 46 us -> none  [the longest x1 34.8 us: on_device(): lax.all_to_all(buckets, 'dec', split_axis=0, concat_axis=2, tiled=True)]
    reduce_sum x6 -> x1, other arithmetic: 19.8 us -> 0.1 us  [visibility_bias(): visible_count = jnp.sum(jnp.where(match, reach[:, :, None], 0), axis=1)]
    all_gather x2 -> x0, blocking collectives: 15.9 us -> none  [the longest x1 8.65 us: on_device(): piece_keys = lax.all_gather(pool_keys, 'pre', axis=0, tiled=True)]
    while x13 -> x0, local copies, waits for them, and re-layouts: 5.93 us -> none
    unnamed x11 -> x12, local copies, waits for them, and re-layouts: 2.98 us -> 7.42 us
  transfers between devices with their start and end apart: 1 -> 0, of which waited for: 1 -> 0; matrix products, arithmetic and copies ran while one was open for 1% -> 0% of each run, Pallas kernels for 0% -> 0%
where the time goes in v1:
time: 181 us
  Pallas kernels  168 us (93%)
  local copies, waits for them, and re-layouts  9.92 us (5%)
  other arithmetic  2.03 us (1%)
    pallas_call x1, Pallas kernels, project(): pl.pallas_call(functools.partial(project_kernel, n_dec, fused), out_shape...  114 us
    pallas_call x1, Pallas kernels, exchange(): pl.pallas_call(functools.partial(exchange_kernel, n_pre, n_dec), out_shap...  29.4 us
    pallas_call x1, Pallas kernels, attention(): pl.pallas_call(attention_kernel, out_shape=jax.ShapeDtypeStruct(queries.s...  24.9 us
    unnamed x12, local copies, waits for them, and re-layouts  7.42 us

profile of v1, /device:TPU:0, one launch (start us, length us, event | category | flops | bytes accessed | tf_op | source)
XLA Modules:
  0.0 180.6 jit_solution(6094052718438258144)
XLA Ops:
  0.6 0.7 dynamic_slice.11
  1.4 0.7 dynamic_slice.9
  2.1 0.1 iota_compare_fusion.1
  2.2 0.8 subtract_clamp_fusion
  3.0 0.1 select_reduce_fusion
  3.1 0.1 lt.36
  3.2 1.0 slice_bitcast_fusion.3
  4.1 1.1 select_select_fusion.bucket_ref
  5.2 29.4 %exchange.1 = (bf16[16,128,256]{2,1,0:T(8,128)(2,1)}, bf16[4,128,512]{2,1,0:T(8,128)(2,1)}) custom-call(bf16[4,128,256]{2,1,0:T(8,128)(2,1)} %pool_ref.1, bf16[8,128,256]{2,1,0:T(8,128)(2,1)} %select_select_fusion.bucket_ref), custom_call_target="tpu_custom_call" | custom-call | tf_op jit(solution)/shard_map/exchange/pallas_call | solution.py:112
  34.6 0.0 copy-start.1
  34.6 1.2 copy-done.1
  35.8 0.0 copy-start.2
  35.8 1.2 copy-done.2
  37.0 0.0 copy-start.3
  37.0 0.9 copy-done.3
  38.0 0.0 copy-start.4
  38.0 24.9 %attention.1.refs_0_ = bf16[4,128,1024]{2,1,0:T(8,128)(2,1)S(1)} custom-call(bf16[4,128,1024]{2,1,0:T(8,128)(2,1)S(1)} %copy-done.1, bf16[4,128,256]{2,1,0:T(8,128)(2,1)S(1)} %copy-done.3, bf16[16,128,256]{2,1,0:T(8,128)(2,1)S(1)} %copy-done.2, f32[4,1,2048]{2,1,0:T(1,128)S(1)} %compare_select_fusion.bias_ref), custom_call_target="tpu_custom_call" | custom-call | tf_op jit(solution)/shard_map/attention/pallas_call | solution.py:189
  62.9 0.0 copy-start
  62.9 1.0 copy-done
  63.8 113.7 %project.1 = bf16[4,128,1024]{2,1,0:T(8,128)(2,1)} custom-call(bf16[4,128,1024]{2,1,0:T(8,128)(2,1)} %copy-done, bf16[1024,8192]{1,0:T(8,128)(2,1)} %refs_1_.1), custom_call_target="tpu_custom_call" | custom-call | tf_op jit(solution)/shard_map/project/pallas_call | solution.py:324
  177.5 2.3 %copy.11 = bf16[4,128,1024]{2,1,0:T(8,128)(2,1)} copy(bf16[4,128,1024]{2,1,0:T(8,128)(2,1)} %project.1) | data formatting | bytes 2097152
  179.8 0.0 copy-done.4
  179.8 0.8 copy.12
  (4 shorter events, 0.0 us)
Async XLA Ops:
  34.6 1.2 copy-start.1
  35.8 1.2 copy-start.2
  37.0 0.9 copy-start.3
  38.0 141.8 %copy-start.4 = (bf16[4,128,512]{2,1,0:T(8,128)(2,1)S(1)}, bf16[4,128,512]{2,1,0:T(8,128)(2,1)}, u32[]{:S(2)}) copy-start(bf16[4,128,512]{2,1,0:T(8,128)(2,1)} %get-tuple-element.19) | copy-start | bytes 1572868
  62.9 1.0 copy-start

commit v2 on v0

v2 whole, which is shorter than its diff:
```python
import functools
import math

import jax
import jax.numpy as jnp
from jax import lax
from jax.experimental import pallas as pl
from jax.experimental.pallas import tpu as pltpu
from jax.sharding import PartitionSpec as P

HD = 128
MASKED = -1e30
SCALE = HD**-0.5 * math.log2(math.e)
MESH = pl.DeviceIdType.MESH
VMEM = pl.BlockSpec(memory_space=pltpu.VMEM)


def from_partner(value, axis, stride):
    mask = 2**stride
    pairs = [(source, source ^ mask) for source in range(lax.axis_size(axis))]
    return lax.ppermute(value, axis, pairs)


def visibility_bias(lists, counts, page_count, page_len):
    slots = lists.shape[1]
    page_ids = jnp.arange(page_count, dtype=jnp.int32)
    reach = jnp.clip(
        counts[:, None] - jnp.arange(slots, dtype=jnp.int32)[None, :] * page_len, 0, page_len
    )
    match = lists[:, :, None] == page_ids[None, None, :]
    visible_count = jnp.sum(jnp.where(match, reach[:, :, None], 0), axis=1)
    tokens = jnp.arange(page_len, dtype=jnp.int32)
    allowed = tokens[None, None, :] < visible_count[:, :, None]
    allowed = allowed.reshape(lists.shape[0], 1, page_count * page_len)
    return jnp.where(allowed, 0.0, MASKED).astype(jnp.float32)


def load_values(pool_ref, values):
    pages, page_len, _ = pool_ref.shape
    values[:, :HD] = pool_ref[:, :, HD:].reshape(pages * page_len, HD)
    values[:, HD:] = jnp.ones((pages * page_len, HD), values.dtype)


def attend(branch, q_ref, own_ref, pool_ref, bias_ref, values, result_ref):
    pages, page_len, _ = pool_ref.shape
    heads = q_ref.shape[2] // HD
    pair = 2
    keys = pool_ref[:, :, :HD].reshape(pages * page_len, HD)
    own_keys = own_ref[branch, :, :HD]
    own_values = own_ref[branch, :, HD:]
    own_values = jnp.concatenate([own_values, jnp.ones_like(own_values)], 1)
    row = lax.broadcasted_iota(jnp.int32, (page_len, page_len), 0)
    col = lax.broadcasted_iota(jnp.int32, (page_len, page_len), 1)
    causal = jnp.where(col <= row, 0.0, MASKED)
    causal = jnp.concatenate([causal] * pair, 0)
    bias = bias_ref[branch]
    nt = (((1,), (1,)), ((), ()))

    def group(g, carry):
        start = pl.multiple_of(g * pair * HD, pair * HD)
        q = q_ref[branch, :, pl.ds(start, pair * HD)]
        q = jnp.concatenate([q[:, i * HD : (i + 1) * HD] for i in range(pair)], 0)
        far = lax.dot_general(q, keys, nt, preferred_element_type=jnp.float32) + bias
        near = lax.dot_general(q, own_keys, nt, preferred_element_type=jnp.float32) + causal
        top = jnp.maximum(
            jnp.max(far, axis=-1, keepdims=True), jnp.max(near, axis=-1, keepdims=True)
        )
        top = top * SCALE
        far = jnp.exp2(far * SCALE - top).astype(jnp.bfloat16)
        near = jnp.exp2(near * SCALE - top).astype(jnp.bfloat16)
        out = jnp.dot(far, values[...], preferred_element_type=jnp.float32)
        out = out + jnp.dot(near, own_values, preferred_element_type=jnp.float32)
        out = (out[:, :HD] / out[:, HD:]).astype(jnp.bfloat16)
        for i in range(pair):
            result_ref[branch, :, pl.ds(start + i * HD, HD)] = out[
                i * page_len : (i + 1) * page_len
            ]
        return carry

    lax.fori_loop(0, heads // pair, group, 0)


def bits_of(index, count):
    return [lax.rem(index // 2**k, 2) for k in range(count)]


def flipped(bits, rel):
    total = 0
    for k, bit in enumerate(bits):
        total = total + 2**k * (1 - bit if rel // 2**k % 2 else bit)
    return total


def halving(order):
    stages = []
    for s, bit in enumerate(order):
        done = [2**k for k in order[:s]]
        rest = [2**k for k in order[s + 1 :]]
        rels = [2**bit]
        for mask in reversed(rest):
            rels = [r + mask for r in rels] + rels
        stages.append([(r, bit, [r + m for m in done]) for r in rels])
    stages.append([(0, None, [2**k for k in order])])
    return stages


def layer_kernel(
    n_pre,
    n_dec,
    cuts,
    pool_ref,
    bucket_ref,
    q_hbm,
    own_hbm,
    bias_ref,
    w_ref,
    out_ref,
    pages_ref,
    all_ref,
    q_ref,
    own_ref,
    values,
    attn,
    wv,
    sent,
    got,
    load_sem,
    wsem,
    psend,
    precv,
    bsend,
    brecv,
    ssem,
    rsem,
):
    pre = lax.axis_index("pre")
    dec = lax.axis_index("dec")
    branches, page_len, cols = out_ref.shape
    count = pool_ref.shape[0]
    width = bucket_ref.shape[2]
    ratio = n_dec // n_pre
    chips = n_pre // 2
    chip = pre // 2
    core = lax.rem(pre, 2)
    log = n_dec.bit_length() - 1
    bits = bits_of(dec, log)

    def block_of(device):
        return pl.ds(device * count, count)

    def across(k):
        return pltpu.make_async_remote_copy(
            src_ref=pool_ref,
            dst_ref=all_ref.at[block_of(pre)],
            send_sem=psend.at[k],
            recv_sem=precv.at[k],
            device_id={"pre": lax.rem(chip + k, chips) * 2 + core},
            device_id_type=MESH,
        )

    def beside(k):
        where = all_ref.at[block_of(lax.rem(chip + chips - k, chips) * 2 + core)]
        return pltpu.make_async_remote_copy(
            src_ref=pool_ref if k == 0 else where,
            dst_ref=where,
            send_sem=psend.at[chips + k],
            recv_sem=precv.at[chips + k],
            device_id={"pre": chip * 2 + 1 - core},
            device_id_type=MESH,
        )

    for k in range(1, chips):
        across(k).start()
    beside(0).start()
    loads = [
        pltpu.make_async_copy(pool_ref, all_ref.at[block_of(pre)], load_sem.at[0]),
        pltpu.make_async_copy(q_hbm, q_ref, load_sem.at[1]),
        pltpu.make_async_copy(own_hbm, own_ref, load_sem.at[2]),
    ]
    for copy in loads:
        copy.start()

    def load(rel):
        start = pl.multiple_of(flipped(bits, rel) * cols, cols)
        return pltpu.make_async_copy(w_ref.at[:, pl.ds(start, cols)], wv.at[rel], wsem.at[rel])

    for rel in range(n_dec):
        load(rel).start()

    home = dec // ratio
    part = lax.rem(dec, ratio)
    column = pl.multiple_of(part * width, 128)

    def bucket_copy(k):
        owner = lax.rem(dec + k, n_dec)
        return pltpu.make_async_remote_copy(
            src_ref=bucket_ref.at[owner],
            dst_ref=pages_ref.at[pre, :, pl.ds(column, width)],
            send_sem=bsend.at[k],
            recv_sem=brecv.at[pre, part],
            device_id={"pre": home, "dec": owner},
            device_id_type=MESH,
        )

    for k in range(1, chips):
        across(k).wait_recv()
        beside(k).start()

    for k in range(1, n_dec):
        bucket_copy(k).start()

    @pl.when(home == pre)
    def _():
        pltpu.make_async_copy(
            bucket_ref.at[dec], pages_ref.at[pre, :, pl.ds(column, width)], brecv.at[pre, part]
        ).start()

    @pl.when(home != pre)
    def _():
        bucket_copy(0).start()

    for copy in loads:
        copy.wait()
    for k in range(chips):
        beside(k).wait_recv()
    load_values(all_ref, values)

    def piece(ref, rel, b, cut):
        return ref.at[rel, b, :, pl.ds(cuts[cut][0], cuts[cut][1])]

    def term_copy(rel, bit, b, cut):
        return pltpu.make_async_remote_copy(
            src_ref=piece(sent, rel, b, cut),
            dst_ref=piece(got, rel, b, cut),
            send_sem=ssem.at[cut, rel, b],
            recv_sem=rsem.at[cut, rel, b],
            device_id={"dec": flipped(bits, 2**bit)},
            device_id_type=MESH,
        )

    plans = [halving(order) for _, _, order in cuts]

    def senders(cut):
        return [(rel, bit) for stage in plans[cut][:-1] for rel, bit, _ in stage]

    bit_of = [dict(senders(cut)) for cut in range(len(cuts))]

    def run_stage(stage, b):
        for cut, (begin, size, _) in enumerate(cuts):
            for rel, bit, parts in plans[cut][stage]:
                for other in parts:
                    term_copy(other, bit_of[cut][other], b, cut).wait_recv()
                step = math.gcd(size, 256)

                def tile(i, carry, rel=rel, begin=begin, parts=parts, step=step, bit=bit):
                    at = pl.ds(pl.multiple_of(begin + i * step, step), step)
                    total = jnp.dot(
                        attn[b], wv[rel, :, at], preferred_element_type=jnp.float32
                    )
                    for other in parts:
                        total = total + got[other, b, :, at].astype(jnp.float32)
                    if bit is None:
                        out_ref[b, :, at] = total.astype(jnp.bfloat16)
                    else:
                        sent[rel, b, :, at] = total.astype(jnp.bfloat16)
                    return carry

                lax.fori_loop(0, size // step, tile, 0)
                if bit is not None:
                    term_copy(rel, bit, b, cut).start()

    def turn(i, carry):
        @pl.when(i < branches)
        def _():
            attend(i, q_ref, own_ref, all_ref, bias_ref, values, attn)

        @pl.when(i == 0)
        def _():
            for rel in range(n_dec):
                load(rel).wait()

        for stage in range(log + 1):
            @pl.when(jnp.logical_and(i >= stage, i < branches + stage))
            def _(stage=stage):
                run_stage(stage, i - stage)

        return carry

    lax.fori_loop(0, branches + log, turn, 0)

    def drain(b, carry):
        for cut in range(len(cuts)):
            for rel, bit in senders(cut):
                term_copy(rel, bit, b, cut).wait_send()
        return carry

    lax.fori_loop(0, branches, drain, 0)
    for k in range(1, chips):
        across(k).wait_send()
    for k in range(chips):
        beside(k).wait_send()
    for k in range(1, n_dec):
        bucket_copy(k).wait_send()

    @pl.when(home != pre)
    def _():
        bucket_copy(0).wait_send()

    for source in range(n_pre):
        for spot in range(ratio):
            where = pages_ref.at[source, :, pl.ds(spot * width, width)]
            pltpu.make_async_copy(where, where, brecv.at[source, spot]).wait()


def layer(pool, buckets, queries, own, bias, weight, n_pre, n_dec):
    branches, page_len, depth = queries.shape
    count = pool.shape[0]
    cols = weight.shape[1] // n_dec
    ratio = n_dec // n_pre
    log = n_dec.bit_length() - 1
    straight = tuple(range(log))
    other = (1, 0) + straight[2:]
    quarter = cols // 4
    cuts = ((0, quarter, other), (quarter, cols - quarter, straight))
    bf16 = jnp.bfloat16
    anywhere = pl.BlockSpec(memory_space=pl.ANY)
    return pl.pallas_call(
        functools.partial(layer_kernel, n_pre, n_dec, cuts),
        out_shape=(
            jax.ShapeDtypeStruct((branches, page_len, cols), bf16),
            jax.ShapeDtypeStruct((n_pre, page_len, ratio * buckets.shape[2]), bf16),
        ),
        in_specs=[anywhere] * 4 + [VMEM, anywhere],
        out_specs=(VMEM, VMEM),
        scratch_shapes=[
            pltpu.VMEM((count * n_pre,) + pool.shape[1:], bf16),
            pltpu.VMEM(queries.shape, bf16),
            pltpu.VMEM(own.shape, bf16),
            pltpu.VMEM((count * n_pre * page_len, 2 * HD), bf16),
            pltpu.VMEM(queries.shape, bf16),
            pltpu.VMEM((n_dec, depth, cols), bf16),
            pltpu.VMEM((n_dec, branches, page_len, cols), bf16),
            pltpu.VMEM((n_dec, branches, page_len, cols), bf16),
            pltpu.SemaphoreType.DMA((3,)),
            pltpu.SemaphoreType.DMA((n_dec,)),
            pltpu.SemaphoreType.DMA((n_pre,)),
            pltpu.SemaphoreType.DMA((n_pre,)),
            pltpu.SemaphoreType.DMA((n_dec,)),
            pltpu.SemaphoreType.DMA((n_pre, ratio)),
            pltpu.SemaphoreType.DMA((2, n_dec, branches)),
            pltpu.SemaphoreType.DMA((2, n_dec, branches)),
        ],
        compiler_params=pltpu.CompilerParams(
            has_side_effects=True, vmem_limit_bytes=62 * 2**20
        ),
        name="layer",
    )(pool, buckets, queries, own, bias, weight)


def on_device(
    queries, branch_kv, pool_kv, page_lists, anc_len, dec_owner, output_projection_weight
):
    n_pre = lax.axis_size("pre")
    n_dec = lax.axis_size("dec")
    pre_idx = lax.axis_index("pre")
    dec_idx = lax.axis_index("dec")
    branch_count, page_len, _ = queries.shape
    kv_cols = pool_kv.shape[2]
    if kv_cols < 2 * HD:
        other_pool, other_own = from_partner((pool_kv, branch_kv), "dec", 0)
        first_half = dec_idx % 2 == 0
        pool = jnp.where(
            first_half,
            jnp.concatenate([pool_kv, other_pool], 2),
            jnp.concatenate([other_pool, pool_kv], 2),
        )
        own = jnp.where(
            first_half,
            jnp.concatenate([branch_kv, other_own], 2),
            jnp.concatenate([other_own, branch_kv], 2),
        )
    else:
        pool, own = pool_kv, branch_kv

    start = pre_idx * branch_count
    my_lists = lax.dynamic_slice_in_dim(page_lists, start, branch_count, 0)
    my_counts = lax.dynamic_slice_in_dim(anc_len, start, branch_count, 0)
    owners = lax.dynamic_slice_in_dim(dec_owner, start, branch_count, 0)
    onehot = owners[:, None] == jnp.arange(n_dec, dtype=jnp.int32)[None, :]
    buckets = jnp.zeros((n_dec,) + branch_kv.shape[1:], branch_kv.dtype)
    for b in range(branch_count):
        buckets = jnp.where(onehot[b][:, None, None], branch_kv[b][None], buckets)

    bias = visibility_bias(my_lists, my_counts, pool.shape[0] * n_pre, page_len)
    layer_out, decode_pages = layer(
        pool, buckets, queries, own, bias, output_projection_weight, n_pre, n_dec
    )
    return (layer_out, decode_pages)


def solution(mesh):
    in_specs = (
        P("pre", None, "dec"),
        P("pre", None, "dec"),
        P("pre", None, "dec"),
        P(),
        P(),
        P(),
        P("dec", None),
    )
    out_specs = (P("pre", None, "dec"), P("dec", None, "pre"))
    return jax.shard_map(
        on_device, mesh=mesh, in_specs=in_specs, out_specs=out_specs, check_vma=False
    )
```

time: 276 us -> 143 us (0.52)
  Pallas kernels: 0 us -> 133 us
  waiting for transfers between devices: 113 us -> 0 us
  blocking collectives: 61.9 us -> 0 us
  matrix products: 54.6 us -> 0 us
  other arithmetic: 20.1 us -> 2.64 us
  between operations: 14.2 us -> 0.66 us
  local copies, waits for them, and re-layouts: 11.6 us -> 6.62 us
    pallas_call x0 -> x1, Pallas kernels: none -> 133 us  [layer(): pl.pallas_call(functools.partial(layer_kernel, n_pre, n_dec, cuts), out_s...]
    reduce_scatter x1 -> x0, waiting for transfers between devices: 113 us -> none  [on_device(): lax.psum_scatter(exponent_term.astype(jnp.bfloat16), 'dec', scatter_dimen...]
    dot_general x12 -> x0, matrix products: 54.6 us -> none  [the longest x5 21 us: merge_score_block(): jnp.einsum(form, weights.astype(jnp.bfloat16), values, preferred_element_...]
    all_to_all x2 -> x0, blocking collectives: 46 us -> none  [the longest x1 34.8 us: on_device(): lax.all_to_all(buckets, 'dec', split_axis=0, concat_axis=2, tiled=True)]
    reduce_sum x6 -> x1, other arithmetic: 19.8 us -> 0.1 us  [visibility_bias(): visible_count = jnp.sum(jnp.where(match, reach[:, :, None], 0), axis=1)]
    all_gather x2 -> x0, blocking collectives: 15.9 us -> none  [the longest x1 8.65 us: on_device(): piece_keys = lax.all_gather(pool_keys, 'pre', axis=0, tiled=True)]
    while x13 -> x0, local copies, waits for them, and re-layouts: 5.93 us -> none
  transfers between devices with their start and end apart: 1 -> 0, of which waited for: 1 -> 0; matrix products, arithmetic and copies ran while one was open for 1% -> 0% of each run, Pallas kernels for 0% -> 0%
where the time goes in v2:
time: 143 us
  Pallas kernels  133 us (93%)
  local copies, waits for them, and re-layouts  6.62 us (5%)
  other arithmetic  2.64 us (2%)
    pallas_call x1, Pallas kernels, layer(): pl.pallas_call(functools.partial(layer_kernel, n_pre, n_dec, cuts), out_s...  133 us
    unnamed x2, local copies, waits for them, and re-layouts  4.13 us

profile of v2, /device:TPU:0, one launch (start us, length us, event | category | flops | bytes accessed | tf_op | source)
XLA Modules:
  0.0 142.5 jit_solution(17790889470997706160)
XLA Ops:
  0.6 0.7 dynamic_slice.11
  1.4 0.7 dynamic_slice.9
  2.1 0.1 iota_compare_fusion.1
  2.2 0.8 subtract_clamp_fusion
  3.0 0.1 select_reduce_fusion
  3.1 0.1 lt.36
  3.1 0.7 compare_select_fusion.bias_ref
  3.8 1.0 slice_bitcast_fusion.3
  4.7 1.1 select_select_fusion.bucket_ref
  5.8 132.6 %layer.1 = (bf16[4,128,1024]{2,1,0:T(8,128)(2,1)}, bf16[4,128,512]{2,1,0:T(8,128)(2,1)}) custom-call(bf16[4,128,256]{2,1,0:T(8,128)(2,1)} %pool_ref.1, bf16[8,128,256]{2,1,0:T(8,128)(2,1)} %select_select_fusion.bucket_ref, bf16[4,128,1024]{2,1,0:T(8,128)(2,1)} %q_hbm.1, bf16[4,128,256]{2,1,0:T(8,128)(2,1)} %own_hbm.1, ...), custom_call_target="tpu_custom_call" | custom-call | tf_op jit(solution)/shard_map/layer/pallas_call | solution.py:327
  138.4 2.3 %copy.11 = bf16[4,128,1024]{2,1,0:T(8,128)(2,1)} copy(bf16[4,128,1024]{2,1,0:T(8,128)(2,1)} %get-tuple-element.14) | data formatting | bytes 2097152
  140.6 1.9 %copy.12 = bf16[4,128,512]{2,1,0:T(8,128)(2,1)} copy(bf16[4,128,512]{2,1,0:T(8,128)(2,1)} %get-tuple-element.15) | data formatting | bytes 1048576
  (3 shorter events, 0.0 us)

commit v3 on v2

--- a/solution.py
+++ b/solution.py
@@ -250,7 +250,7 @@
             for rel, bit, parts in plans[cut][stage]:
                 for other in parts:
                     term_copy(other, bit_of[cut][other], b, cut).wait_recv()
-                step = math.gcd(size, 256)
+                step = math.gcd(size, 512)
 
                 def tile(i, carry, rel=rel, begin=begin, parts=parts, step=step, bit=bit):
                     at = pl.ds(pl.multiple_of(begin + i * step, step), step)
@@ -320,8 +320,8 @@
     log = n_dec.bit_length() - 1
     straight = tuple(range(log))
     other = (1, 0) + straight[2:]
-    quarter = cols // 4
-    cuts = ((0, quarter, other), (quarter, cols - quarter, straight))
+    part = cols // 2
+    cuts = ((0, part, other), (part, cols - part, straight))
     bf16 = jnp.bfloat16
     anywhere = pl.BlockSpec(memory_space=pl.ANY)
     return pl.pallas_call(

time: 143 us -> 134 us (0.937)
  Pallas kernels: 133 us -> 124 us
    pallas_call x1, Pallas kernels: 133 us -> 124 us  [layer(): pl.pallas_call(functools.partial(layer_kernel, n_pre, n_dec, cuts), out_s...]
where the time goes in v3:
time: 134 us
  Pallas kernels  124 us (93%)
  local copies, waits for them, and re-layouts  6.62 us (5%)
  other arithmetic  2.64 us (2%)
    pallas_call x1, Pallas kernels, layer(): pl.pallas_call(functools.partial(layer_kernel, n_pre, n_dec, cuts), out_s...  124 us
    unnamed x2, local copies, waits for them, and re-layouts  4.13 us

profile of v3, /device:TPU:0, one launch (start us, length us, event | category | flops | bytes accessed | tf_op | source)
XLA Modules:
  0.0 133.7 jit_solution(11036966867719568794)
XLA Ops:
  0.6 0.7 dynamic_slice.11
  1.4 0.7 dynamic_slice.9
  2.1 0.1 iota_compare_fusion.1
  2.2 0.8 subtract_clamp_fusion
  3.0 0.1 select_reduce_fusion
  3.1 0.1 lt.36
  3.1 0.7 compare_select_fusion.bias_ref
  3.8 1.0 slice_bitcast_fusion.3
  4.7 1.1 select_select_fusion.bucket_ref
  5.8 123.7 %layer.1 = (bf16[4,128,1024]{2,1,0:T(8,128)(2,1)}, bf16[4,128,512]{2,1,0:T(8,128)(2,1)}) custom-call(bf16[4,128,256]{2,1,0:T(8,128)(2,1)} %pool_ref.1, bf16[8,128,256]{2,1,0:T(8,128)(2,1)} %select_select_fusion.bucket_ref, bf16[4,128,1024]{2,1,0:T(8,128)(2,1)} %q_hbm.1, bf16[4,128,256]{2,1,0:T(8,128)(2,1)} %own_hbm.1, ...), custom_call_target="tpu_custom_call" | custom-call | tf_op jit(solution)/shard_map/layer/pallas_call | solution.py:327
  129.5 2.3 %copy.11 = bf16[4,128,1024]{2,1,0:T(8,128)(2,1)} copy(bf16[4,128,1024]{2,1,0:T(8,128)(2,1)} %get-tuple-element.14) | data formatting | bytes 2097152
  131.8 1.9 %copy.12 = bf16[4,128,512]{2,1,0:T(8,128)(2,1)} copy(bf16[4,128,512]{2,1,0:T(8,128)(2,1)} %get-tuple-element.15) | data formatting | bytes 1048576
  (3 shorter events, 0.0 us)

commit v4 on v3

--- a/solution.py
+++ b/solution.py
@@ -246,8 +246,9 @@
     bit_of = [dict(senders(cut)) for cut in range(len(cuts))]
 
     def run_stage(stage, b):
-        for cut, (begin, size, _) in enumerate(cuts):
-            for rel, bit, parts in plans[cut][stage]:
+        for turns in zip(*[plan[stage] for plan in plans]):
+            for cut, (rel, bit, parts) in enumerate(turns):
+                begin, size, _ = cuts[cut]
                 for other in parts:
                     term_copy(other, bit_of[cut][other], b, cut).wait_recv()
                 step = math.gcd(size, 512)

time: 134 us -> 134 us (level)
  no operation moved by 1% of the time
where the time goes in v4:
time: 134 us
  Pallas kernels  124 us (93%)
  local copies, waits for them, and re-layouts  6.62 us (5%)
  other arithmetic  2.64 us (2%)
    pallas_call x1, Pallas kernels, layer(): pl.pallas_call(functools.partial(layer_kernel, n_pre, n_dec, cuts), out_s...  124 us
    unnamed x2, local copies, waits for them, and re-layouts  4.13 us

profile of v4, /device:TPU:0, one launch (start us, length us, event | category | flops | bytes accessed | tf_op | source)
XLA Modules:
  0.0 133.7 jit_solution(9418763693532403088)
XLA Ops:
  0.6 0.7 dynamic_slice.11
  1.4 0.7 dynamic_slice.9
  2.1 0.1 iota_compare_fusion.1
  2.2 0.8 subtract_clamp_fusion
  3.0 0.1 select_reduce_fusion
  3.1 0.1 lt.36
  3.1 0.7 compare_select_fusion.bias_ref
  3.8 1.0 slice_bitcast_fusion.3
  4.7 1.1 select_select_fusion.bucket_ref
  5.8 123.7 %layer.1 = (bf16[4,128,1024]{2,1,0:T(8,128)(2,1)}, bf16[4,128,512]{2,1,0:T(8,128)(2,1)}) custom-call(bf16[4,128,256]{2,1,0:T(8,128)(2,1)} %pool_ref.1, bf16[8,128,256]{2,1,0:T(8,128)(2,1)} %select_select_fusion.bucket_ref, bf16[4,128,1024]{2,1,0:T(8,128)(2,1)} %q_hbm.1, bf16[4,128,256]{2,1,0:T(8,128)(2,1)} %own_hbm.1, ...), custom_call_target="tpu_custom_call" | custom-call | tf_op jit(solution)/shard_map/layer/pallas_call | solution.py:328
  129.5 2.3 %copy.11 = bf16[4,128,1024]{2,1,0:T(8,128)(2,1)} copy(bf16[4,128,1024]{2,1,0:T(8,128)(2,1)} %get-tuple-element.14) | data formatting | bytes 2097152
  131.8 1.9 %copy.12 = bf16[4,128,512]{2,1,0:T(8,128)(2,1)} copy(bf16[4,128,512]{2,1,0:T(8,128)(2,1)} %get-tuple-element.15) | data formatting | bytes 1048576
  (3 shorter events, 0.0 us)
